TPU v7x, 128 devices: a whole 4x4x4 slice. The times are simulated.
128 devices in a mesh: board: 8 (over y, z_lo), crate: 16 (over x, z_hi, core).
Axes of the slice: x: 4, y: 4, z: 4 (z_hi: 2, z_lo: 2; z = z_hi * 2 + z_lo), core: 2. Of those that a mesh axis runs over, the one named last changes fastest.
Arguments:
- voltages: bfloat16 [1024, 530432], P(('board', 'crate')), may hold values from -6 to 6
- gains: float32 [2, 1024, 256], P(None, ('board', 'crate')), may hold values from -4 to 4
- channels: int32 [256], replicated, may hold values from 0 to 1023, as said below
Outputs:
- visibilities: float32 [2, 256, 1024, 1024], P(None, ('board', 'crate'))
Inputs may be any that keep to these rules, and one draw needn't show every extreme that they name: `channels`: distinct transform bins below half of 2048, in no particular order; bin 0 and the highest such bin are always among them.
All inputs are finite; a program needn't handle non-finite values.
Results may differ from a plain program's by a relative error of at most 0.0056.
Values may be sent and summed in bfloat16 or wider, within the bound.
No kernel may reach another device: no remote copies, remote signals or barrier semaphores. Data moves between devices by JAX's collectives and lax.ppermute only.
A program may use at most 128 MiB of HBM per device.

v0:
```python
import math

import jax
import jax.numpy as jnp
from jax import lax
from jax.experimental import pallas as pl
from jax.experimental.pallas import tpu as pltpu
from jax.sharding import PartitionSpec as P

NFFT = 2048
TAPS = 4
LANES = 128
CHUNK = 32
COARSE = 64


def make_window(taps_count, length):
    index = jnp.arange(taps_count * length).astype(jnp.float32)
    centred = (index - taps_count * length / 2 + 0.5) / length
    hamming = 0.54 - 0.46 * jnp.cos(2.0 * jnp.pi * index / (taps_count * length - 1))
    return (jnp.sinc(centred) * hamming).reshape(taps_count, length)


def phasor(rows, channels):
    phase = (rows * channels) & (NFFT - 1)
    quarter = NFFT // 4
    turn = (phase + quarter // 2) // quarter
    angle = (phase - turn * quarter).astype(jnp.float32) * (2.0 * math.pi / NFFT)
    square = angle * angle
    sine = angle * (
        1.0 + square * (-1 / 6 + square * (1 / 120 + square * (-1 / 5040 + square * (1 / 362880))))
    )
    cosine = 1.0 + square * (
        -1 / 2
        + square * (1 / 24 + square * (-1 / 720 + square * (1 / 40320 - square * (1 / 3628800))))
    )
    swap = (turn & 1) == 1
    turned_cos = jnp.where(swap, sine, cosine)
    turned_sin = jnp.where(swap, cosine, sine)
    cos_sign = jnp.where(((turn + 1) & 2) == 2, -1.0, 1.0)
    sin_sign = jnp.where((turn & 2) == 2, -1.0, 1.0)
    return turned_cos * cos_sign, turned_sin * sin_sign


def front_kernel(v_hbm, window, channels, gains, out, volts, table, filtered, raw, turned, sems):
    inputs = out.shape[2]
    kept = out.shape[0]
    frames = out.shape[3]
    chunks = frames // CHUNK
    span = CHUNK * NFFT
    rows = CHUNK * inputs
    tail = (TAPS - 1) * NFFT

    def piece(k):
        start = 0 if k == 0 else tail + k * span
        size = span + tail if k == 0 else span
        return pltpu.make_async_copy(
            v_hbm.at[:, pl.ds(start, size)], volts.at[:, pl.ds(start, size)], sems.at[k]
        )

    for k in range(chunks):
        piece(k).start()

    scale = 1.0 / math.sqrt(NFFT)
    for half in range(kept // LANES):
        lanes = pl.ds(half * LANES, LANES)
        bins = channels[:, lanes]
        fine_cos, fine_sin = phasor(lax.broadcasted_iota(jnp.int32, (COARSE, LANES), 0), bins)
        fine_cos, fine_sin = fine_cos * scale, fine_sin * scale
        steps = NFFT // COARSE
        coarse_cos_all, coarse_sin_all = phasor(
            lax.broadcasted_iota(jnp.int32, (steps, LANES), 0) * COARSE, bins
        )

        for a in range(steps):
            coarse_cos = coarse_cos_all[a : a + 1]
            coarse_sin = coarse_sin_all[a : a + 1]
            at = pl.ds(a * COARSE, COARSE)
            table[at, lanes] = (fine_cos * coarse_cos - fine_sin * coarse_sin).astype(
                jnp.bfloat16
            )
            table[at, pl.ds(kept + half * LANES, LANES)] = (
                -(fine_sin * coarse_cos + fine_cos * coarse_sin)
            ).astype(jnp.bfloat16)

    for k in range(chunks):
        piece(k).wait()

        @pl.loop(0, NFFT // LANES)
        def _(j):
            lane = pl.multiple_of(j * LANES, LANES)
            taps = [
                jnp.broadcast_to(window[t : t + 1, pl.ds(lane, LANES)], (inputs, LANES))
                for t in range(TAPS)
            ]

            def load(f):
                at = pl.multiple_of(lane + (k * CHUNK + f) * NFFT, LANES)
                return volts[:, pl.ds(at, LANES)].astype(jnp.float32)

            held = [load(f) for f in range(TAPS - 1)]
            for f in range(0, CHUNK, 2):
                pair = []
                for g in (f, f + 1):
                    held.append(load(g + TAPS - 1))
                    total = taps[0] * held[0]
                    for t in range(1, TAPS):
                        total = total + taps[t] * held[t]
                    held.pop(0)
                    pair.append(total)
                filtered[pl.ds(f * inputs, 2 * inputs), pl.ds(lane, LANES)] = jnp.concatenate(
                    pair, axis=0
                ).astype(jnp.bfloat16)

        product = jnp.dot(filtered[...], table[...], preferred_element_type=jnp.float32)
        for q in range(2 * kept // LANES):
            raw[q, pl.ds(k * rows, rows), :] = product[:, q * LANES : (q + 1) * LANES]

    for half in range(kept // LANES):
        lanes = pl.ds(half * LANES, LANES)
        for block in range(frames // LANES):
            for i in range(inputs):
                at = pl.ds(block * LANES * inputs + i, LANES, stride=inputs)
                gain_real = gains[0, i : i + 1, lanes]
                gain_imag = gains[1, i : i + 1, lanes]
                real = raw[half, at, :]
                imag = raw[half + kept // LANES, at, :]
                turned[0, pl.ds(i, LANES, stride=inputs), :] = (
                    gain_real * real - gain_imag * imag
                ).T
                turned[1, pl.ds(i, LANES, stride=inputs), :] = (
                    gain_real * imag + gain_imag * real
                ).T
            for part in range(2):
                out[
                    pl.ds(half * LANES, LANES), part, :, pl.ds(block * LANES, LANES)
                ] = turned[part].reshape(LANES, inputs, LANES).astype(jnp.bfloat16)


def front_end(voltages, gains, channels):
    inputs, samples = voltages.shape
    frames = samples // NFFT - TAPS + 1
    kept = channels.shape[0]
    window = make_window(TAPS, NFFT)
    vmem = pl.BlockSpec(memory_space=pltpu.VMEM)
    return pl.pallas_call(
        front_kernel,
        out_shape=jax.ShapeDtypeStruct((kept, 2, inputs, frames), jnp.bfloat16),
        in_specs=[pl.BlockSpec(memory_space=pltpu.HBM), vmem, vmem, vmem],
        out_specs=vmem,
        scratch_shapes=[
            pltpu.VMEM((inputs, samples), jnp.bfloat16),
            pltpu.VMEM((NFFT, 2 * kept), jnp.bfloat16),
            pltpu.VMEM((CHUNK * inputs, NFFT), jnp.bfloat16),
            pltpu.VMEM((2 * kept // LANES, frames * inputs, LANES), jnp.float32),
            pltpu.VMEM((2, LANES * inputs, LANES), jnp.float32),
            pltpu.SemaphoreType.DMA((frames // CHUNK,)),
        ],
        compiler_params=pltpu.CompilerParams(vmem_limit_bytes=60 * 2**20),
        cost_estimate=pl.CostEstimate(
            flops=4 * frames * inputs * NFFT * kept,
            bytes_accessed=2 * inputs * samples,
            transcendentals=0,
        ),
        name="front_end",
    )(voltages, window, channels.reshape(1, kept), gains)


def correlate_kernel(spectra, out, rows):
    sources, _, _, inputs, frames = spectra.shape
    total = sources * inputs
    width = out.shape[3]
    step = pl.program_id(1)

    @pl.when(step == 0)
    def _():
        c = pl.program_id(0)
        real = spectra[:, c, 0].reshape(total, frames)
        imag = spectra[:, c, 1].reshape(total, frames)
        rows[pl.ds(0, total), pl.ds(0, frames)] = real
        rows[pl.ds(0, total), pl.ds(frames, frames)] = imag
        rows[pl.ds(total, total), pl.ds(0, frames)] = imag
        rows[pl.ds(total, total), pl.ds(frames, frames)] = -real

    at = pl.ds(pl.multiple_of(step * width, width), width)
    product = lax.dot_general(
        rows[...],
        rows[at, :],
        (((1,), (1,)), ((), ())),
        preferred_element_type=jnp.float32,
    )
    out[0, 0] = product[:total] / frames
    out[1, 0] = product[total:] / frames


def correlate(spectra):
    sources, owned, _, inputs, frames = spectra.shape
    total = sources * inputs
    width = 256
    return pl.pallas_call(
        correlate_kernel,
        grid=(owned, total // width),
        out_shape=jax.ShapeDtypeStruct((2, owned, total, total), jnp.float32),
        in_specs=[pl.BlockSpec(memory_space=pltpu.VMEM)],
        out_specs=pl.BlockSpec((2, 1, total, width), lambda c, r: (0, c, 0, r)),
        scratch_shapes=[pltpu.VMEM((2 * total, 2 * frames), jnp.bfloat16)],
        compiler_params=pltpu.CompilerParams(
            dimension_semantics=("arbitrary", "arbitrary"), vmem_limit_bytes=40 * 2**20
        ),
        cost_estimate=pl.CostEstimate(
            flops=8 * owned * total * total * frames,
            bytes_accessed=8 * owned * total * total,
            transcendentals=0,
        ),
        name="correlate",
    )(spectra)


def solution(mesh):
    devices = mesh.size
    axes = ("board", "crate")

    def local(voltages, gains, channels):
        spectra = front_end(voltages, gains, channels)
        kept = spectra.shape[0]
        split = spectra.reshape(devices, kept // devices, *spectra.shape[1:])
        return correlate(lax.all_to_all(split, axes, 0, 0, tiled=True))

    placed = (P(axes, None), P(None, axes, None), P())
    return jax.shard_map(
        local,
        mesh=mesh,
        in_specs=placed,
        out_specs=P(None, axes, None, None),
        check_vma=False,
    )
```

profile of v0, /device:TPU:1, one launch (start us, length us, event | category | flops | bytes accessed | tf_op | source)
XLA Modules:
  0.0 67.8 jit_solution(17878141185330526146)
XLA Ops:
  0.0 0.9 %fusion.5.window = f32[4,2048]{1,0:T(4,128)} fusion(), kind=kLoop, calls=%fused_computation.11 | loop fusion | flops 344064 | bytes 32768 | tf_op jit(solution)/shard_map/mul | solution.py:21
  0.9 16.4 %front_end.1 = bf16[256,2,8,256]{3,2,1,0:T(8,128)(2,1)} custom-call(bf16[8,530432]{1,0:T(8,128)(2,1)} %v_hbm.1, f32[4,2048]{1,0:T(4,128)} %fusion.5.window, s32[1,256]{1,0:T(1,128)} %bitcast.3, f32[2,8,256]{2,1,0:T(8,128)} %gains.1), custom_call_target="tpu_custom_call" | custom-call | flops 4294967296 | bytes 8486912 | tf_op jit(solution)/shard_map/front_end/pallas_call | solution.py:146
  17.3 41.2 %all_to_all.5.spectra = bf16[128,2,2,8,256]{4,3,2,1,0:T(8,128)(2,1)S(1)} all-to-all(bf16[128,2,2,8,256]{4,3,2,1,0:T(8,128)(2,1)} %bitcast.2), channel_id=1, replica_groups=mesh['board'=8,'crate'=16] {'board','crate'}, dimensions={0} | all-to-all | bytes 4194304 | tf_op jit(solution)/shard_map/all_to_all | solution.py:227
  58.5 9.3 %correlate.1 = f32[2,2,1024,1024]{3,2,1,0:T(8,128)} custom-call(bf16[128,2,2,8,256]{4,3,2,1,0:T(8,128)(2,1)S(1)} %all_to_all.5.spectra), custom_call_target="tpu_custom_call" | custom-call | flops 4294967296 | bytes 16777216 | tf_op jit(solution)/shard_map/correlate/pallas_call | solution.py:200
where the time goes:
time: 68.1 us; the launch traced here: 67.8 us
  blocking collectives  41.2 us (60%)
  Pallas kernels  25.6 us (38%)
  other arithmetic  0.92 us (1%)
    all_to_all x1, blocking collectives, local(): return correlate(lax.all_to_all(split, axes, 0, 0, tiled=True))  41.2 us
    pallas_call x1, Pallas kernels, front_end(): pl.pallas_call(front_kernel, out_shape=jax.ShapeDtypeStruct((kept, 2, inp...  16.4 us
    pallas_call x1, Pallas kernels, correlate(): pl.pallas_call(correlate_kernel, grid=(owned, total // width), out_shape=...  9.29 us

commit v1 on v0

v1 whole, which is shorter than its diff:
```python
import math

import jax
import jax.numpy as jnp
import numpy as np
from jax import lax
from jax.experimental import pallas as pl
from jax.experimental.pallas import tpu as pltpu
from jax.sharding import PartitionSpec as P

NFFT = 2048
TAPS = 4
LANES = 128
WIDE = 256
CHUNK = 32
COARSE = 64


def make_window(taps_count, length):
    index = np.arange(taps_count * length, dtype=np.float64)
    centred = (index - taps_count * length / 2 + 0.5) / length
    hamming = 0.54 - 0.46 * np.cos(2.0 * np.pi * index / (taps_count * length - 1))
    return (np.sinc(centred) * hamming).reshape(taps_count, length).astype(np.float32)


def phasor(rows, channels):
    phase = (rows * channels) & (NFFT - 1)
    quarter = NFFT // 4
    turn = (phase + quarter // 2) // quarter
    angle = (phase - turn * quarter).astype(jnp.float32) * (2.0 * math.pi / NFFT)
    square = angle * angle
    sine = angle * (
        1.0 + square * (-1 / 6 + square * (1 / 120 + square * (-1 / 5040 + square * (1 / 362880))))
    )
    cosine = 1.0 + square * (
        -1 / 2
        + square * (1 / 24 + square * (-1 / 720 + square * (1 / 40320 - square * (1 / 3628800))))
    )
    swap = (turn & 1) == 1
    turned_cos = jnp.where(swap, sine, cosine)
    turned_sin = jnp.where(swap, cosine, sine)
    cos_sign = jnp.where(((turn + 1) & 2) == 2, -1.0, 1.0)
    sin_sign = jnp.where((turn & 2) == 2, -1.0, 1.0)
    return turned_cos * cos_sign, turned_sin * sin_sign


def front_kernel(
    v_hbm, window_hbm, channels_hbm, gains_hbm, out,
    volts, window, channels, gains, table, even, odd, raw, turned, sems, small_sems,
):
    inputs = out.shape[2]
    kept = out.shape[0]
    frames = out.shape[3]
    chunks = frames // CHUNK
    span = CHUNK * NFFT
    rows = CHUNK * inputs
    tail = (TAPS - 1) * NFFT
    parts = kept // LANES

    def piece(k):
        at = pl.ds(tail + k * span, span)
        return pltpu.make_async_copy(v_hbm.at[:, at], volts.at[:, at], sems.at[k])

    head = pltpu.make_async_copy(
        v_hbm.at[:, pl.ds(0, tail)], volts.at[:, pl.ds(0, tail)], sems.at[chunks]
    )
    small = [
        pltpu.make_async_copy(source, target, small_sems.at[n])
        for n, (source, target) in enumerate(
            ((channels_hbm, channels), (window_hbm, window), (gains_hbm, gains))
        )
    ]
    small[0].start()
    head.start()
    small[1].start()
    for k in range(chunks):
        piece(k).start()
    small[2].start()

    scale = 1.0 / math.sqrt(NFFT)
    steps = NFFT // 2 // COARSE
    small[0].wait()
    for part in range(parts):
        lanes = pl.ds(part * LANES, LANES)
        others = pl.ds(kept + part * LANES, LANES)
        bins = channels[:, lanes]
        fine_cos, fine_sin = phasor(lax.broadcasted_iota(jnp.int32, (COARSE, LANES), 0), bins)
        fine_cos, fine_sin = fine_cos * scale, fine_sin * -scale
        coarse_cos, coarse_sin = phasor(
            lax.broadcasted_iota(jnp.int32, (steps, LANES), 0) * COARSE, bins
        )
        sign = jnp.where((bins & 1) == 1, -1.0, 1.0).astype(jnp.bfloat16)
        for a in range(steps):
            cos_a = coarse_cos[a : a + 1]
            sin_a = coarse_sin[a : a + 1]
            real = (fine_cos * cos_a + fine_sin * sin_a).astype(jnp.bfloat16)
            imag = (fine_sin * cos_a - fine_cos * sin_a).astype(jnp.bfloat16)
            table[pl.ds(a * COARSE, COARSE), lanes] = real
            table[pl.ds(a * COARSE, COARSE), others] = imag
            table[pl.ds(NFFT // 2 + a * COARSE, COARSE), lanes] = real * sign
            table[pl.ds(NFFT // 2 + a * COARSE, COARSE), others] = imag * sign

    def filter_tile(k, target, lane):
        taps = [
            jnp.broadcast_to(window[t : t + 1, pl.ds(lane, WIDE)], (inputs, WIDE))
            for t in range(TAPS)
        ]

        def load(f):
            at = (k * CHUNK + f) * NFFT + lane
            if not isinstance(at, int):
                at = pl.multiple_of(at, LANES)
            return volts[:, pl.ds(at, WIDE)].astype(jnp.float32)

        held = [load(f) for f in range(TAPS - 1)]
        for f in range(0, CHUNK, 2):
            pair = []
            for g in (f, f + 1):
                held.append(load(g + TAPS - 1))
                total = taps[0] * held[0]
                for t in range(1, TAPS):
                    total = total + taps[t] * held[t]
                held.pop(0)
                pair.append(total)
            target[pl.ds(f * inputs, 2 * inputs), pl.ds(lane, WIDE)] = jnp.concatenate(
                pair, axis=0
            ).astype(jnp.bfloat16)

    def transform(k, source):
        product = jnp.dot(source[...], table[...], preferred_element_type=jnp.float32)
        at = pl.ds(k * rows, rows)
        for q in range(2 * parts):
            raw[q, at, :] = product[:, q * LANES : (q + 1) * LANES]

    def both(k, source, target):
        transform(k, source)
        for j in range(NFFT // WIDE):
            filter_tile(k + 1, target, j * WIDE)

    small[1].wait()
    head.wait()
    piece(0).wait()

    @pl.loop(0, NFFT // WIDE)
    def _(j):
        filter_tile(0, even, pl.multiple_of(j * WIDE, WIDE))

    small[2].wait()
    early = chunks // 2
    for k in range(1, early):
        piece(k).wait()
    for k in range(chunks - 1):
        if k + 1 == early:
            for later in range(early, chunks):
                piece(later).wait()
        both(k, *((even, odd) if k % 2 == 0 else (odd, even)))
    transform(chunks - 1, even if chunks % 2 == 1 else odd)

    for part in range(parts):
        lanes = pl.ds(part * LANES, LANES)
        for block in range(frames // LANES):
            for i in range(inputs):
                at = pl.ds(block * LANES * inputs + i, LANES, stride=inputs)
                gain_real = gains[0, i : i + 1, lanes]
                gain_imag = gains[1, i : i + 1, lanes]
                real = raw[part, at, :]
                imag = raw[part + parts, at, :]
                turned[0, pl.ds(i, LANES, stride=inputs), :] = (
                    gain_real * real - gain_imag * imag
                ).T
                turned[1, pl.ds(i, LANES, stride=inputs), :] = (
                    gain_real * imag + gain_imag * real
                ).T
            for side in range(2):
                out[
                    pl.ds(part * LANES, LANES), side, :, pl.ds(block * LANES, LANES)
                ] = turned[side].reshape(LANES, inputs, LANES).astype(jnp.bfloat16)


def front_end(voltages, gains, channels):
    inputs, samples = voltages.shape
    frames = samples // NFFT - TAPS + 1
    kept = channels.shape[0]
    window = jnp.asarray(make_window(TAPS, NFFT))
    hbm = pl.BlockSpec(memory_space=pltpu.HBM)
    return pl.pallas_call(
        front_kernel,
        out_shape=jax.ShapeDtypeStruct((kept, 2, inputs, frames), jnp.bfloat16),
        in_specs=[hbm] * 4,
        out_specs=pl.BlockSpec(memory_space=pltpu.VMEM),
        scratch_shapes=[
            pltpu.VMEM((inputs, samples), jnp.bfloat16),
            pltpu.VMEM((TAPS, NFFT), jnp.float32),
            pltpu.VMEM((1, kept), jnp.int32),
            pltpu.VMEM((2, inputs, kept), jnp.float32),
            pltpu.VMEM((NFFT, 2 * kept), jnp.bfloat16),
            pltpu.VMEM((CHUNK * inputs, NFFT), jnp.bfloat16),
            pltpu.VMEM((CHUNK * inputs, NFFT), jnp.bfloat16),
            pltpu.VMEM((2 * kept // LANES, frames * inputs, LANES), jnp.float32),
            pltpu.VMEM((2, LANES * inputs, LANES), jnp.float32),
            pltpu.SemaphoreType.DMA((frames // CHUNK + 1,)),
            pltpu.SemaphoreType.DMA((3,)),
        ],
        compiler_params=pltpu.CompilerParams(vmem_limit_bytes=50 * 2**20),
        cost_estimate=pl.CostEstimate(
            flops=4 * frames * inputs * NFFT * kept,
            bytes_accessed=2 * inputs * samples,
            transcendentals=0,
        ),
        name="front_end",
    )(
        voltages,
        *(
            pltpu.with_memory_space_constraint(x, pltpu.HBM)
            for x in (window, channels.reshape(1, kept), gains)
        ),
    )


def correlate_kernel(spectra, out, rows, blocks, sems):
    sources, owned, _, inputs, frames = spectra.shape
    total = sources * inputs
    side = blocks.shape[-1]
    across = total // side
    contract = (((1,), (1,)), ((), ()))

    for c in range(owned):
        real = spectra[:, c, 0].reshape(total, frames)
        imag = spectra[:, c, 1].reshape(total, frames)
        rows[c, 0, :, pl.ds(0, frames)] = real
        rows[c, 0, :, pl.ds(frames, frames)] = imag
        rows[c, 1, :, pl.ds(0, frames)] = imag
        rows[c, 1, :, pl.ds(frames, frames)] = -real

    def copies(c, a, b, slot):
        every = []
        for n, (row, column) in enumerate(((a, b), (b, a)) if a != b else ((a, b),)):
            every.append(
                pltpu.make_async_copy(
                    blocks.at[slot, n],
                    out.at[:, c, pl.ds(row * side, side), pl.ds(column * side, side)],
                    sems.at[slot, n],
                )
            )
        return every

    slots = blocks.shape[0]
    flying = []
    for c in range(owned):
        for b in range(across):
            for a in range(b, across):
                step = len(flying)
                slot = step % slots
                if step >= slots:
                    for copy in flying[step - slots]:
                        copy.wait()
                weights = rows[c, 0, pl.ds(b * side, side), :]
                for part in range(2):
                    block = lax.dot_general(
                        rows[c, part, pl.ds(a * side, side), :],
                        weights,
                        contract,
                        preferred_element_type=jnp.float32,
                    ) / frames
                    blocks[slot, 0, part] = block
                    if a != b:
                        mirror = block.T
                        blocks[slot, 1, part] = mirror if part == 0 else -mirror
                started = copies(c, a, b, slot)
                for copy in started:
                    copy.start()
                flying.append(started)
    for started in flying[-slots:]:
        for copy in started:
            copy.wait()


def correlate(spectra):
    sources, owned, _, inputs, frames = spectra.shape
    total = sources * inputs
    side = 256
    slots = 6
    return pl.pallas_call(
        correlate_kernel,
        out_shape=jax.ShapeDtypeStruct((2, owned, total, total), jnp.float32),
        in_specs=[pl.BlockSpec(memory_space=pltpu.VMEM)],
        out_specs=pl.BlockSpec(memory_space=pltpu.HBM),
        scratch_shapes=[
            pltpu.VMEM((owned, 2, total, 2 * frames), jnp.bfloat16),
            pltpu.VMEM((slots, 2, 2, side, side), jnp.float32),
            pltpu.SemaphoreType.DMA((slots, 2)),
        ],
        compiler_params=pltpu.CompilerParams(vmem_limit_bytes=40 * 2**20),
        cost_estimate=pl.CostEstimate(
            flops=8 * owned * total * total * frames,
            bytes_accessed=8 * owned * total * total,
            transcendentals=0,
        ),
        name="correlate",
    )(spectra)


def solution(mesh):
    devices = mesh.size
    axes = ("board", "crate")

    def local(voltages, gains, channels):
        spectra = front_end(voltages, gains, channels)
        kept = spectra.shape[0]
        split = spectra.reshape(devices, kept // devices, *spectra.shape[1:])
        return correlate(lax.all_to_all(split, axes, 0, 0, tiled=True))

    placed = (P(axes, None), P(None, axes, None), P())
    return jax.shard_map(
        local,
        mesh=mesh,
        in_specs=placed,
        out_specs=P(None, axes, None, None),
        check_vma=False,
    )
```

time: 68.1 us -> 60.7 us (0.89)
  Pallas kernels: 25.6 us -> 19.4 us
  other arithmetic: 0.92 us -> 0 us
    pallas_call x1, Pallas kernels: 16.4 us -> 11.3 us  [front_end(): pl.pallas_call(front_kernel, out_shape=jax.ShapeDtypeStruct((kept, 2, inp...]
    pallas_call x1, Pallas kernels: 9.29 us -> 8.1 us  [correlate(): pl.pallas_call(correlate_kernel, out_shape=jax.ShapeDtypeStruct((2, owned...]
    mul x1 -> x0, other arithmetic: 0.92 us -> none  [make_window(): return (jnp.sinc(centred) * hamming).reshape(taps_count, length)]
where the time goes in v1:
time: 60.7 us; the launch traced here: 60.6 us
  blocking collectives  41 us (68%)
  Pallas kernels  19.4 us (32%)
    all_to_all x1, blocking collectives, local(): return correlate(lax.all_to_all(split, axes, 0, 0, tiled=True))  41 us
    pallas_call x1, Pallas kernels, front_end(): pl.pallas_call(front_kernel, out_shape=jax.ShapeDtypeStruct((kept, 2, inp...  11.3 us
    pallas_call x1, Pallas kernels, correlate(): pl.pallas_call(correlate_kernel, out_shape=jax.ShapeDtypeStruct((2, owned...  8.1 us

profile of v1, /device:TPU:1, one launch (start us, length us, event | category | flops | bytes accessed | tf_op | source)
XLA Modules:
  0.0 60.6 jit_solution(8354025514592640851)
XLA Ops:
  0.0 11.3 %front_end.1 = bf16[256,2,8,256]{3,2,1,0:T(8,128)(2,1)S(1)} custom-call(bf16[8,530432]{1,0:T(8,128)(2,1)} %v_hbm.1, f32[4,2048]{1,0:T(4,128)} %constant.2.clone.window_hbm, s32[1,256]{1,0:T(1,128)} %bitcast.3, f32[2,8,256]{2,1,0:T(8,128)} %gains_hbm.1), custom_call_target="tpu_custom_call" | custom-call | flops 4294967296 | bytes 8486912 | tf_op jit(solution)/shard_map/front_end/pallas_call | solution.py:186
  11.3 41.0 %all_to_all.5.spectra = bf16[128,2,2,8,256]{4,3,2,1,0:T(8,128)(2,1)S(1)} all-to-all(bf16[128,2,2,8,256]{4,3,2,1,0:T(8,128)(2,1)S(1)} %bitcast.2), channel_id=1, replica_groups=mesh['board'=8,'crate'=16] {'board','crate'}, dimensions={0} | all-to-all | bytes 4194304 | tf_op jit(solution)/shard_map/all_to_all | solution.py:311
  52.3 8.1 %correlate.1 = f32[2,2,1024,1024]{3,2,1,0:T(8,128)} custom-call(bf16[128,2,2,8,256]{4,3,2,1,0:T(8,128)(2,1)S(1)} %all_to_all.5.spectra), custom_call_target="tpu_custom_call" | custom-call | flops 4294967296 | bytes 16777216 | tf_op jit(solution)/shard_map/correlate/pallas_call | solution.py:283

commit v2 on v1

--- a/solution.py
+++ b/solution.py
@@ -46,7 +46,7 @@
 
 def front_kernel(
     v_hbm, window_hbm, channels_hbm, gains_hbm, out,
-    volts, window, channels, gains, table, even, odd, raw, turned, sems, small_sems,
+    volts, window, channels, gains, last_gains, table, first, second, third, raw, turned, sems, small_sems,
 ):
     inputs = out.shape[2]
     kept = out.shape[0]
@@ -67,7 +67,12 @@
     small = [
         pltpu.make_async_copy(source, target, small_sems.at[n])
         for n, (source, target) in enumerate(
-            ((channels_hbm, channels), (window_hbm, window), (gains_hbm, gains))
+            (
+                (channels_hbm, channels),
+                (window_hbm, window),
+                (gains_hbm, gains),
+                (gains_hbm, last_gains),
+            )
         )
     ]
     small[0].start()
@@ -76,14 +81,15 @@
     for k in range(chunks):
         piece(k).start()
     small[2].start()
+    small[3].start()
 
     scale = 1.0 / math.sqrt(NFFT)
     steps = NFFT // 2 // COARSE
     small[0].wait()
     for part in range(parts):
-        lanes = pl.ds(part * LANES, LANES)
-        others = pl.ds(kept + part * LANES, LANES)
-        bins = channels[:, lanes]
+        lanes = pl.ds(2 * part * LANES, LANES)
+        others = pl.ds((2 * part + 1) * LANES, LANES)
+        bins = channels[:, pl.ds(part * LANES, LANES)]
         fine_cos, fine_sin = phasor(lax.broadcasted_iota(jnp.int32, (COARSE, LANES), 0), bins)
         fine_cos, fine_sin = fine_cos * scale, fine_sin * -scale
         coarse_cos, coarse_sin = phasor(
@@ -126,55 +132,63 @@
                 pair, axis=0
             ).astype(jnp.bfloat16)
 
-    def transform(k, source):
-        product = jnp.dot(source[...], table[...], preferred_element_type=jnp.float32)
+    def transform(k, pieces):
+        source = slots[k % len(slots)]
+        width = 2 * kept // pieces
         at = pl.ds(k * rows, rows)
-        for q in range(2 * parts):
-            raw[q, at, :] = product[:, q * LANES : (q + 1) * LANES]
-
-    def both(k, source, target):
-        transform(k, source)
-        for j in range(NFFT // WIDE):
-            filter_tile(k + 1, target, j * WIDE)
-
+        for n in range(pieces):
+            product = jnp.dot(
+                source[...],
+                table[:, n * width : (n + 1) * width],
+                preferred_element_type=jnp.float32,
+            )
+            for q in range(width // LANES):
+                raw[n * width // LANES + q, at, :] = product[:, q * LANES : (q + 1) * LANES]
+
+    slots = (first, second, third)
+    ahead = len(slots) - 1
     small[1].wait()
     head.wait()
-    piece(0).wait()
-
-    @pl.loop(0, NFFT // WIDE)
-    def _(j):
-        filter_tile(0, even, pl.multiple_of(j * WIDE, WIDE))
+    for k in range(ahead):
+        piece(k).wait()
+
+        @pl.loop(0, NFFT // WIDE)
+        def _(j):
+            filter_tile(k, slots[k], pl.multiple_of(j * WIDE, WIDE))
 
     small[2].wait()
-    early = chunks // 2
-    for k in range(1, early):
+    for k in range(ahead, chunks):
         piece(k).wait()
-    for k in range(chunks - 1):
-        if k + 1 == early:
-            for later in range(early, chunks):
-                piece(later).wait()
-        both(k, *((even, odd) if k % 2 == 0 else (odd, even)))
-    transform(chunks - 1, even if chunks % 2 == 1 else odd)
-
-    for part in range(parts):
+    for k in range(chunks):
+        transform(k, parts if k == chunks - 1 else 1)
+        if k + ahead < chunks:
+            for j in range(NFFT // WIDE):
+                filter_tile(k + ahead, slots[(k + ahead) % len(slots)], j * WIDE)
+
+    def turn(part, block, gains):
         lanes = pl.ds(part * LANES, LANES)
-        for block in range(frames // LANES):
-            for i in range(inputs):
-                at = pl.ds(block * LANES * inputs + i, LANES, stride=inputs)
-                gain_real = gains[0, i : i + 1, lanes]
-                gain_imag = gains[1, i : i + 1, lanes]
-                real = raw[part, at, :]
-                imag = raw[part + parts, at, :]
-                turned[0, pl.ds(i, LANES, stride=inputs), :] = (
-                    gain_real * real - gain_imag * imag
-                ).T
-                turned[1, pl.ds(i, LANES, stride=inputs), :] = (
-                    gain_real * imag + gain_imag * real
-                ).T
-            for side in range(2):
-                out[
-                    pl.ds(part * LANES, LANES), side, :, pl.ds(block * LANES, LANES)
-                ] = turned[side].reshape(LANES, inputs, LANES).astype(jnp.bfloat16)
+        for i in range(inputs):
+            at = pl.ds(block * LANES * inputs + i, LANES, stride=inputs)
+            gain_real = gains[0, i : i + 1, lanes]
+            gain_imag = gains[1, i : i + 1, lanes]
+            real = raw[2 * part, at, :]
+            imag = raw[2 * part + 1, at, :]
+            turned[0, pl.ds(i, LANES, stride=inputs), :] = (
+                gain_real * real - gain_imag * imag
+            ).T
+            turned[1, pl.ds(i, LANES, stride=inputs), :] = (
+                gain_real * imag + gain_imag * real
+            ).T
+        for side in range(2):
+            out[pl.ds(part * LANES, LANES), side, :, pl.ds(block * LANES, LANES)] = (
+                turned[side].reshape(LANES, inputs, LANES).astype(jnp.bfloat16)
+            )
+
+    turns = [(part, block) for block in range(frames // LANES) for part in range(parts)]
+    for part, block in turns[:-1]:
+        turn(part, block, gains)
+    small[3].wait()
+    turn(*turns[-1], last_gains)
 
 
 def front_end(voltages, gains, channels):
@@ -192,14 +206,13 @@
             pltpu.VMEM((inputs, samples), jnp.bfloat16),
             pltpu.VMEM((TAPS, NFFT), jnp.float32),
             pltpu.VMEM((1, kept), jnp.int32),
-            pltpu.VMEM((2, inputs, kept), jnp.float32),
+            *[pltpu.VMEM((2, inputs, kept), jnp.float32)] * 2,
             pltpu.VMEM((NFFT, 2 * kept), jnp.bfloat16),
-            pltpu.VMEM((CHUNK * inputs, NFFT), jnp.bfloat16),
-            pltpu.VMEM((CHUNK * inputs, NFFT), jnp.bfloat16),
+            *[pltpu.VMEM((CHUNK * inputs, NFFT), jnp.bfloat16)] * 3,
             pltpu.VMEM((2 * kept // LANES, frames * inputs, LANES), jnp.float32),
             pltpu.VMEM((2, LANES * inputs, LANES), jnp.float32),
             pltpu.SemaphoreType.DMA((frames // CHUNK + 1,)),
-            pltpu.SemaphoreType.DMA((3,)),
+            pltpu.SemaphoreType.DMA((4,)),
         ],
         compiler_params=pltpu.CompilerParams(vmem_limit_bytes=50 * 2**20),
         cost_estimate=pl.CostEstimate(
@@ -244,16 +257,11 @@
             )
         return every
 
-    slots = blocks.shape[0]
     flying = []
     for c in range(owned):
         for b in range(across):
             for a in range(b, across):
-                step = len(flying)
-                slot = step % slots
-                if step >= slots:
-                    for copy in flying[step - slots]:
-                        copy.wait()
+                slot = len(flying)
                 weights = rows[c, 0, pl.ds(b * side, side), :]
                 for part in range(2):
                     block = lax.dot_general(
@@ -270,7 +278,7 @@
                 for copy in started:
                     copy.start()
                 flying.append(started)
-    for started in flying[-slots:]:
+    for started in flying:
         for copy in started:
             copy.wait()
 
@@ -279,7 +287,8 @@
     sources, owned, _, inputs, frames = spectra.shape
     total = sources * inputs
     side = 256
-    slots = 6
+    across = total // side
+    slots = owned * across * (across + 1) // 2
     return pl.pallas_call(
         correlate_kernel,
         out_shape=jax.ShapeDtypeStruct((2, owned, total, total), jnp.float32),
@@ -290,7 +299,7 @@
             pltpu.VMEM((slots, 2, 2, side, side), jnp.float32),
             pltpu.SemaphoreType.DMA((slots, 2)),
         ],
-        compiler_params=pltpu.CompilerParams(vmem_limit_bytes=40 * 2**20),
+        compiler_params=pltpu.CompilerParams(vmem_limit_bytes=48 * 2**20),
         cost_estimate=pl.CostEstimate(
             flops=8 * owned * total * total * frames,
             bytes_accessed=8 * owned * total * total,

time: 60.7 us -> 58.2 us (0.959)
  Pallas kernels: 19.4 us -> 17.1 us
    pallas_call x1, Pallas kernels: 8.1 us -> 6.67 us  [correlate(): pl.pallas_call(correlate_kernel, out_shape=jax.ShapeDtypeStruct((2, owned...]
    pallas_call x1, Pallas kernels: 11.3 us -> 10.4 us  [front_end(): pl.pallas_call(front_kernel, out_shape=jax.ShapeDtypeStruct((kept, 2, inp...]
where the time goes in v2:
time: 58.2 us; the launch traced here: 58.1 us
  blocking collectives  41 us (70%)
  Pallas kernels  17.1 us (29%)
    all_to_all x1, blocking collectives, local(): return correlate(lax.all_to_all(split, axes, 0, 0, tiled=True))  41 us
    pallas_call x1, Pallas kernels, front_end(): pl.pallas_call(front_kernel, out_shape=jax.ShapeDtypeStruct((kept, 2, inp...  10.4 us
    pallas_call x1, Pallas kernels, correlate(): pl.pallas_call(correlate_kernel, out_shape=jax.ShapeDtypeStruct((2, owned...  6.67 us

profile of v2, /device:TPU:1, one launch (start us, length us, event | category | flops | bytes accessed | tf_op | source)
XLA Modules:
  0.0 58.1 jit_solution(2541427653961675494)
XLA Ops:
  0.0 10.4 %front_end.1 = bf16[256,2,8,256]{3,2,1,0:T(8,128)(2,1)S(1)} custom-call(bf16[8,530432]{1,0:T(8,128)(2,1)} %v_hbm.1, f32[4,2048]{1,0:T(4,128)} %constant.2.clone.window_hbm, s32[1,256]{1,0:T(1,128)} %bitcast.3, f32[2,8,256]{2,1,0:T(8,128)} %gains_hbm.1), custom_call_target="tpu_custom_call" | custom-call | flops 4294967296 | bytes 8486912 | tf_op jit(solution)/shard_map/front_end/pallas_call | solution.py:200
  10.5 41.0 %all_to_all.5.spectra = bf16[128,2,2,8,256]{4,3,2,1,0:T(8,128)(2,1)S(1)} all-to-all(bf16[128,2,2,8,256]{4,3,2,1,0:T(8,128)(2,1)S(1)} %bitcast.2), channel_id=1, replica_groups=mesh['board'=8,'crate'=16] {'board','crate'}, dimensions={0} | all-to-all | bytes 4194304 | tf_op jit(solution)/shard_map/all_to_all | solution.py:320
  51.4 6.7 %correlate.1 = f32[2,2,1024,1024]{3,2,1,0:T(8,128)} custom-call(bf16[128,2,2,8,256]{4,3,2,1,0:T(8,128)(2,1)S(1)} %all_to_all.5.spectra), custom_call_target="tpu_custom_call" | custom-call | flops 4294967296 | bytes 16777216 | tf_op jit(solution)/shard_map/correlate/pallas_call | solution.py:292

commit v3 on v2

--- a/solution.py
+++ b/solution.py
@@ -237,7 +237,7 @@
     across = total // side
     contract = (((1,), (1,)), ((), ()))
 
-    for c in range(owned):
+    def arrange(c):
         real = spectra[:, c, 0].reshape(total, frames)
         imag = spectra[:, c, 1].reshape(total, frames)
         rows[c, 0, :, pl.ds(0, frames)] = real
@@ -259,6 +259,7 @@
 
     flying = []
     for c in range(owned):
+        arrange(c)
         for b in range(across):
             for a in range(b, across):
                 slot = len(flying)

time: 58.2 us -> 58.2 us (level)
  no operation moved by 1% of the time
where the time goes in v3:
time: 58.2 us; the launch traced here: 58 us
  blocking collectives  41 us (70%)
  Pallas kernels  17.1 us (29%)
    all_to_all x1, blocking collectives, local(): return correlate(lax.all_to_all(split, axes, 0, 0, tiled=True))  41 us
    pallas_call x1, Pallas kernels, front_end(): pl.pallas_call(front_kernel, out_shape=jax.ShapeDtypeStruct((kept, 2, inp...  10.4 us
    pallas_call x1, Pallas kernels, correlate(): pl.pallas_call(correlate_kernel, out_shape=jax.ShapeDtypeStruct((2, owned...  6.6 us

profile of v3, /device:TPU:1, one launch (start us, length us, event | category | flops | bytes accessed | tf_op | source)
XLA Modules:
  0.0 58.0 jit_solution(16050633177376942570)
XLA Ops:
  0.0 10.4 %front_end.1 = bf16[256,2,8,256]{3,2,1,0:T(8,128)(2,1)S(1)} custom-call(bf16[8,530432]{1,0:T(8,128)(2,1)} %v_hbm.1, f32[4,2048]{1,0:T(4,128)} %constant.2.clone.window_hbm, s32[1,256]{1,0:T(1,128)} %bitcast.3, f32[2,8,256]{2,1,0:T(8,128)} %gains_hbm.1), custom_call_target="tpu_custom_call" | custom-call | flops 4294967296 | bytes 8486912 | tf_op jit(solution)/shard_map/front_end/pallas_call | solution.py:200
  10.5 41.0 %all_to_all.5.spectra = bf16[128,2,2,8,256]{4,3,2,1,0:T(8,128)(2,1)S(1)} all-to-all(bf16[128,2,2,8,256]{4,3,2,1,0:T(8,128)(2,1)S(1)} %bitcast.2), channel_id=1, replica_groups=mesh['board'=8,'crate'=16] {'board','crate'}, dimensions={0} | all-to-all | bytes 4194304 | tf_op jit(solution)/shard_map/all_to_all | solution.py:321
  51.4 6.6 %correlate.1 = f32[2,2,1024,1024]{3,2,1,0:T(8,128)} custom-call(bf16[128,2,2,8,256]{4,3,2,1,0:T(8,128)(2,1)S(1)} %all_to_all.5.spectra), custom_call_target="tpu_custom_call" | custom-call | flops 4294967296 | bytes 16777216 | tf_op jit(solution)/shard_map/correlate/pallas_call | solution.py:293
